TPU v7x, 512 devices: a whole 4x8x8 slice. The times are simulated.
512 devices in a mesh: gx: 32 (over y, x), gy: 16 (over z, core).
Axes of the slice: x: 4, y: 8, z: 8, core: 2. Of those that a mesh axis runs over, the one named last changes fastest.
Arguments:
- water_state: float32 [3, 2048, 8192], P(None, 'gy', 'gx'), may hold values from -0.5 to 1.5, as said below
- bed_level: float32 [2048, 8192], P('gy', 'gx'), may hold values from -0.1 to 0.1
- active_tiles: int32 [1, 16, 64], replicated, may hold values from 0 to 1, as said below
- roughness: int32 [16, 64], replicated, may hold values from 0 to 3
Outputs:
- water_out: float32 [3, 2048, 8192], P(None, 'gy', 'gx')
Inputs may be any that keep to these rules, and one draw needn't show every extreme that they name: `water_state`: entry 0 along the first dimension is the water depth, at least 0.5 everywhere; entries 1 and 2 are the discharges along the columns and along the rows, of magnitude at most 0.5. `active_tiles`: whole blocks of 2 tiles side by side along the columns, starting at multiples of 2, may be off the list together.
All inputs are finite; a program needn't handle non-finite values.
Results may differ from a plain program's by a relative error of at most 0.0003.
Values sent between devices are 32-bit elements; how exact they have to be, the bound alone decides.
No kernel may reach another device: no remote copies, remote signals or barrier semaphores. Data moves between devices by JAX's collectives and lax.ppermute only.
A program may use at most 64 MiB of HBM per device.

v0:
```python
import jax
import jax.numpy as jnp
from jax import lax
from jax.experimental import pallas as pl
from jax.experimental.pallas import tpu as pltpu
from jax.sharding import PartitionSpec as P


GRAVITY = 9.81
SPACING = 2.0
TIME_STEP = 0.1
MANNING = (0.03, 0.06, 0.1, 0.15)

LANES = 128
ROWS = 128
HALO = 4
TOP = 16
STAGED = ROWS + 2 * TOP
RIM = 2
SQRT_G = GRAVITY**0.5
HALF_G = 0.5 * GRAVITY
FLUX_SCALE = 0.5 * TIME_STEP / SPACING
BED_SCALE = TIME_STEP * GRAVITY / (2.0 * SPACING)
DRAG_SCALE = TIME_STEP * GRAVITY
SMALLEST = 1.1754944e-38

OWN, ABOVE, BELOW = (0, 1, 2), (3, 4, 2), (5, 6, 2)
REGIONS = 7

VMEM = pl.BlockSpec(memory_space=pltpu.VMEM)
HBM = pl.BlockSpec(memory_space=pltpu.HBM)

HELD = (12, STAGED, LANES)
MID = (9, STAGED, LANES)
SLOPE = (4, STAGED, LANES)
KNOWN = (8, STAGED, LANES)
FACTORS = (3 * REGIONS, 8, LANES)
STRIP = (16, LANES)
BAND = (16, 3 * LANES)
BLOCK = (3, ROWS, 2 * LANES)
INNER = 16


def swap(x, axis, odd):
    n = lax.axis_size(axis)
    pairs = []
    for i in range(odd, n - 1, 2):
        pairs += [(i, i + 1), (i + 1, i)]
    return lax.ppermute(x, axis, pairs)


def lane_ids(rows):
    return lax.broadcasted_iota(jnp.int32, (rows, LANES), 1)


def row_ids():
    return lax.broadcasted_iota(jnp.int32, (8, LANES), 0)


def strips_kernel(water, bed, msg_b, msg_a, own_b, held, sems):
    even = lax.rem(lax.axis_index("gx"), 2) == 0
    copies = []
    for f in range(4):
        for t in range(2):
            cols = pl.ds(t * LANES, LANES)
            src = water.at[f, :, cols] if f < 3 else bed.at[:, cols]
            dst = held.at[3 * f + t, pl.ds(TOP, ROWS), :]
            copies.append(pltpu.make_async_copy(src, dst, sems.at[len(copies)]))
    for copy in copies:
        copy.start()
    for copy in copies:
        copy.wait()
    group = lane_ids(ROWS) // HALO
    packed = None
    for f in range(4):
        for side in range(2):
            v = held[3 * f + side, TOP : TOP + ROWS, :]
            shift = (4 * f + 20 * side) % LANES
            v = pltpu.roll(v, shift, 1) if shift else v
            packed = v if packed is None else jnp.where(group == f + 4 * side, v, packed)
    across = packed.T
    left, right = across[0:16, :], across[16:32, :]
    msg_a[...] = jnp.where(even, right, left)
    msg_b[...] = jnp.where(even, left, right)
    own_b[...] = jnp.where(even, left, right)


def ahead_kernel(held, active, rough, factors, known, on_flags, levels, sems):
    gx, nx = lax.axis_index("gx"), lax.axis_size("gx")
    gy, ny = lax.axis_index("gy"), lax.axis_size("gy")
    copies = [
        pltpu.make_async_copy(active, on_flags, sems.at[0]),
        pltpu.make_async_copy(rough, levels, sems.at[1]),
    ]
    for copy in copies:
        copy.start()

    def keep_drag(c):
        load = loader(held, c)
        for t in range(2):
            known[6 + t, pl.ds(row_of(c), 8), :] = drag(*(load(f, t, 0) for f in range(3)))

    def ahead(c, previous):
        faces = row_faces(loader(held, c), range(2))
        over = upper_faces(previous, faces)
        for t in range(2):
            for i in range(3):
                known[2 * i + t, pl.ds(row_of(c), 8), :] = faces[t][i] - over[t][i]
        keep_drag(c)
        return faces

    keep_drag(1)
    lax.fori_loop(2, 16, ahead, row_faces(loader(held, 1), range(2)), unroll=2)
    keep_drag(16)
    for copy in copies:
        copy.wait()

    def tile_of(dy, dx):
        row = jnp.clip(gy + dy, 0, ny - 1)
        col = jnp.clip(2 * gx + dx, 0, 2 * nx - 1)
        on = on_flags[0, row, col].astype(jnp.float32)
        level = levels[row, col]
        squares = [DRAG_SCALE * (n * n) for n in MANNING]
        coarse = jnp.where(level == 2, squares[2], squares[3])
        fine = jnp.where(level == 0, squares[0], squares[1])
        return FLUX_SCALE * on, BED_SCALE * on, jnp.where(level < 2, fine, coarse) * on

    low = lane_ids(8) < 64
    sites = [(0, 0), (0, 1), None, (-1, 0), (-1, 1), (1, 0), (1, 1)]
    for region, site in enumerate(sites):
        if site is None:
            ahead, behind = tile_of(0, 2), tile_of(0, -1)
            values = [jnp.where(low, a, b) for a, b in zip(ahead, behind)]
        else:
            values = [jnp.full((8, LANES), v, jnp.float32) for v in tile_of(*site)]
        for i, v in enumerate(values):
            factors[3 * region + i] = v


def rows_kernel(held_in, own_b, got_b, got_a, after, msg_b, msg_a, keep_b, held, stage):
    gx, nx = lax.axis_index("gx"), lax.axis_size("gx")
    even = lax.rem(gx, 2) == 0
    border = jnp.logical_or(gx == 0, gx == nx - 1)
    stage[...] = jnp.zeros_like(stage)
    for f in range(4):
        a = got_a[4 * f : 4 * f + 4, :]
        b = got_b[4 * f : 4 * f + 4, :]
        sign = -1.0 if f == 1 else 1.0
        mirrored = jnp.concatenate(
            [own_b[4 * f + 3 - k : 4 * f + 4 - k, :] for k in range(4)], axis=0
        )
        b = jnp.where(border, sign * mirrored, b)
        stage[8 * f : 8 * f + 4, :] = jnp.where(even, b, a)
        stage[8 * f + 4 : 8 * f + 8, :] = jnp.where(even, a, b)
    upright = stage[...].T
    even_y = lax.rem(lax.axis_index("gy"), 2) == 0
    for f in range(4):
        rim = pltpu.roll(upright, 124 - 8 * f, 1)
        held[3 * f + RIM, TOP : TOP + ROWS, :] = rim
        for t in range(3):
            if t == RIM:
                upper, lower = rim[0:4, :], rim[124:128, :]
            else:
                upper = held_in[3 * f + t, TOP : TOP + 4, :]
                lower = held_in[3 * f + t, TOP + 124 : TOP + 128, :]
            at = (pl.ds(4 * f, 4), pl.ds(t * LANES, LANES))
            msg_a[at] = jnp.where(even_y, lower, upper)
            msg_b[at] = jnp.where(even_y, upper, lower)
            keep_b[at] = jnp.where(even_y, upper, lower)


def side_states(vm, v0, v1, v2):
    d0, d1, d2 = v0 - vm, v1 - v0, v2 - v1
    low, high = jnp.minimum(d1, 0.0), jnp.maximum(d1, 0.0)
    s0 = jnp.minimum(jnp.maximum(d0, low), high)
    s1 = jnp.minimum(jnp.maximum(d2, low), high)
    return v0 + 0.5 * s0, v1 - 0.5 * s1


def side_terms(h, n):
    q = lax.rsqrt(h)
    u = n * (q * q)
    return u, jnp.abs(u) + SQRT_G * (h * q)


def rusanov(left, right):
    (hl, nl, tl), (hr, nr, tr) = left, right
    ul, cl = side_terms(hl, nl)
    ur, cr = side_terms(hr, nr)
    c = jnp.maximum(cl, cr)
    return (
        (nl + nr) - c * (hr - hl),
        (nl * ul + nr * ur) + HALF_G * (hl * hl + hr * hr) - c * (nr - nl),
        (tl * ul + tr * ur) - c * (tr - tl),
    )


def drag(h, p, r):
    square = p * p + r * r
    return square * lax.rsqrt(jnp.maximum(square, SMALLEST)) * jnp.exp(jnp.log(h) * (-7.0 / 3.0))


class Ring:
    def __init__(self):
        lanes = lane_ids(8)
        self.first = lanes == 0
        self.second = lanes < 2
        self.last = lanes == LANES - 1

    def right(self, v, by=1):
        moved = [pltpu.roll(x, by, 1) for x in v]
        edge = self.first if by == 1 else self.second
        return [jnp.where(edge, moved[t - 1], moved[t]) for t in range(3)]

    def left(self, v, count=3):
        moved = [pltpu.roll(x, LANES - 1, 1) for x in v]
        return [jnp.where(self.last, moved[(t + 1) % 3], moved[t]) for t in range(count)]

    def rates(self, h, p, r, count):
        sides = []
        for v in (h, p, r):
            near, far, ahead = self.right(v), self.right(v, 2), self.left(v)
            sides.append([side_states(far[t], near[t], v[t], ahead[t]) for t in range(3)])
        face = [
            rusanov([x[t][0] for x in sides], [x[t][1] for x in sides]) for t in range(3)
        ]
        out = []
        for i in range(3):
            g = [face[t][i] for t in range(3)]
            moved = self.left(g, count)
            out.append([moved[t] - g[t] for t in range(count)])
        return out


def row_faces(load, tiles):
    out = []
    for t in tiles:
        sides = [side_states(*(load(f, t, k) for k in (-1, 0, 1, 2))) for f in (0, 2, 1)]
        out.append(rusanov([s[0] for s in sides], [s[1] for s in sides]))
    return out


def upper_faces(previous, faces):
    bottom = row_ids() == 7
    return [
        tuple(pltpu.roll(jnp.where(bottom, a, b), 1, 0) for a, b in zip(p, n))
        for p, n in zip(previous, faces)
    ]


def row_of(c):
    at = 8 * c + TOP - 8
    return at if isinstance(c, int) else pl.multiple_of(at, 8)


def loader(ref, c):
    base = row_of(c)
    return lambda f, t, k: ref[3 * f + t, pl.ds(base + k, 8), :]


def first_stage(ring, held, factors, mid, slope, regions, c, previous, known=None):
    rows = pl.ds(row_of(c), 8)
    load = loader(held, c)
    faces = row_faces(load, range(3) if known is None else [RIM])
    over = upper_faces(previous, faces)
    downs = [[n - o for n, o in zip(*pair)] for pair in zip(faces, over)]
    if known is not None:
        downs = [[known[2 * i + t, rows, :] for i in range(3)] for t in range(2)] + downs
    h, p, r, b = ([load(f, t, 0) for t in range(3)] for f in range(4))
    along = ring.rates(h, p, r, 3)
    to_left, to_right = ring.right(b), ring.left(b)
    for t in range(3):
        flux, bed, rub = (factors[3 * regions[t] + i] for i in range(3))
        bed_x = bed * (to_right[t] - to_left[t])
        bed_y = bed * (load(3, t, 1) - load(3, t, -1))
        if t != RIM:
            slope[t, rows, :] = bed_x
            slope[2 + t, rows, :] = bed_y
        if known is None or t == RIM:
            res = rub * drag(h[t], p[t], r[t])
        else:
            res = rub * known[6 + t, rows, :]
        down = downs[t]
        mid[t, rows, :] = h[t] - flux * (along[0][t] + down[0])
        mid[3 + t, rows, :] = p[t] - (
            flux * (along[1][t] + down[2]) + (h[t] * bed_x + res * p[t])
        )
        mid[6 + t, rows, :] = r[t] - (
            flux * (along[2][t] + down[1]) + (h[t] * bed_y + res * r[t])
        )
    return faces


def second_stage(ring, held, factors, mid, slope, out, place, c, previous):
    rows = pl.ds(row_of(c), 8)
    load = loader(mid, c)
    faces = row_faces(load, range(2))
    over = upper_faces(previous, faces)
    h, p, r = ([load(f, t, 0) for t in range(3)] for f in range(3))
    along = ring.rates(h, p, r, 2)
    for t in range(2):
        flux, _, rub = (factors[3 * OWN[t] + i] for i in range(3))
        res = rub * drag(h[t], p[t], r[t])
        down = [n - o for n, o in zip(faces[t], over[t])]
        change = (
            flux * (along[0][t] + down[0]),
            flux * (along[1][t] + down[2]) + (h[t] * slope[t, rows, :] + res * p[t]),
            flux * (along[2][t] + down[1]) + (h[t] * slope[2 + t, rows, :] + res * r[t]),
        )
        for f, v in enumerate((h, p, r)):
            start = held[3 * f + t, rows, :]
            out[f, pl.ds(place, 8), pl.ds(t * LANES, LANES)] = 0.5 * ((start + v[t]) - change[f])
    return faces


def inner_section(held, factors, known, mid, slope):
    ring = Ring()

    def first(c, previous):
        return first_stage(ring, held, factors, mid, slope, OWN, c, previous, known)

    lax.fori_loop(2, 16, first, row_faces(loader(held, 1), [RIM]), unroll=2)


def inner_result(held, factors, mid, slope, part):
    ring = Ring()

    def second(c, previous):
        place = pl.multiple_of(8 * c - 8, 8)
        return second_stage(ring, held, factors, mid, slope, part, place, c, previous)

    lax.fori_loop(3, 15, second, row_faces(loader(mid, 2), range(2)), unroll=4)


def odd_kernel(held, factors, known, msg_in, mid, slope, part, msg):
    @pl.when(lax.rem(lax.axis_index("gy"), 2) == 1)
    def _():
        inner_section(held, factors, known, mid, slope)
        inner_result(held, factors, mid, slope, part)


def even_kernel(held, factors, known, msg_in, mid_in, slope_in, mid, slope, msg):
    @pl.when(lax.rem(lax.axis_index("gy"), 2) == 0)
    def _():
        inner_section(held, factors, known, mid, slope)


def rest_kernel(held, factors, mid, slope, part_in, part):
    @pl.when(lax.rem(lax.axis_index("gy"), 2) == 0)
    def _():
        inner_result(held, factors, mid, slope, part)


def outer_kernel(
    held_in, mid_in, slope_in, part, factors, own_b, got_b, got_a, out, held, mid, slope, edge, sems
):
    inner = pl.ds(INNER, ROWS - 2 * INNER)
    copies = [pltpu.make_async_copy(part.at[:, inner, :], out.at[:, inner, :], sems.at[0])]
    for i in range(2):
        src, dst = pl.ds(i * INNER, INNER), pl.ds(i * (ROWS - INNER), INNER)
        copies.append(pltpu.make_async_copy(edge.at[:, src, :], out.at[:, dst, :], sems.at[1 + i]))
    copies[0].start()
    gy, ny = lax.axis_index("gy"), lax.axis_size("gy")
    even_y = lax.rem(gy, 2) == 0
    border = jnp.logical_or(gy == 0, gy == ny - 1)
    for f in range(4):
        for t in range(3):
            cols = slice(t * LANES, (t + 1) * LANES)
            sign = -1.0 if f == 2 else 1.0
            mirrored = jnp.concatenate(
                [own_b[4 * f + 3 - k : 4 * f + 4 - k, cols] for k in range(4)], axis=0
            )
            a = got_a[4 * f : 4 * f + 4, cols]
            b = jnp.where(border, sign * mirrored, got_b[4 * f : 4 * f + 4, cols])
            held[3 * f + t, TOP - 4 : TOP, :] = jnp.where(even_y, b, a)
            held[3 * f + t, TOP + ROWS : TOP + ROWS + 4, :] = jnp.where(even_y, a, b)

    ring = Ring()
    zero = jnp.zeros((8, LANES), jnp.float32)

    def first(c, regions, previous):
        return first_stage(ring, held, factors, mid, slope, regions, c, previous)

    def second(c, place, previous):
        return second_stage(ring, held, factors, mid, slope, edge, place, c, previous)

    first(1, OWN, first(0, ABOVE, [(zero, zero, zero)] * 3))
    first(17, BELOW, first(16, OWN, row_faces(loader(held, 15), range(3))))
    second(2, 8, second(1, 0, row_faces(loader(mid, 0), range(2))))
    copies[1].start()
    second(16, 24, second(15, 16, row_faces(loader(mid, 14), range(2))))
    copies[2].start()
    for copy in copies:
        copy.wait()


def call(kernel, outs, specs, scratch=(), aliases=None, room=4, cost=0, out_specs=None):
    shapes = [jax.ShapeDtypeStruct(s, jnp.float32) for s in outs]
    return pl.pallas_call(
        kernel,
        out_shape=shapes,
        in_specs=specs,
        out_specs=out_specs or [VMEM] * len(shapes),
        scratch_shapes=scratch,
        input_output_aliases=aliases or {},
        compiler_params=pltpu.CompilerParams(vmem_limit_bytes=room << 20),
        cost_estimate=pl.CostEstimate(flops=cost, bytes_accessed=cost, transcendentals=0),
    )


def body(water, bed, active, rough):
    col_b, col_a, own_col, held = call(
        strips_kernel,
        [STRIP, STRIP, STRIP, HELD],
        [HBM] * 2,
        [pltpu.SemaphoreType.DMA((8,))],
    )(*(pltpu.with_memory_space_constraint(x, pltpu.HBM) for x in (water, bed)))
    got_b = swap(col_b, "gx", 1)
    got_a = swap(col_a, "gx", 0)
    factors, known = call(
        ahead_kernel,
        [FACTORS, KNOWN],
        [VMEM, HBM, HBM],
        [
            pltpu.SMEM((1, 16, 64), jnp.int32),
            pltpu.SMEM((16, 64), jnp.int32),
            pltpu.SemaphoreType.DMA((2,)),
        ],
        cost=4_000_000,
    )(held, *(pltpu.with_memory_space_constraint(x, pltpu.HBM) for x in (active, rough)))
    row_b, row_a, own_row, held = call(
        rows_kernel,
        [BAND, BAND, BAND, HELD],
        [VMEM] * 5,
        [pltpu.VMEM((LANES, LANES), jnp.float32)],
        {0: 3},
    )(held, own_col, got_b, got_a, factors)
    mid, slope, part, row_b = call(
        odd_kernel, [MID, SLOPE, BLOCK, BAND], [VMEM] * 4, aliases={3: 3}, room=8, cost=10_000_000
    )(held, factors, known, row_b)
    down_b = swap(row_b, "gy", 1)
    mid, slope, row_a = call(
        even_kernel,
        [MID, SLOPE, BAND],
        [VMEM] * 6,
        aliases={4: 0, 5: 1, 3: 2},
        room=8,
        cost=10_000_000,
    )(held, factors, known, row_a, mid, slope)
    down_a = swap(row_a, "gy", 0)
    part = call(rest_kernel, [BLOCK], [VMEM] * 5, aliases={4: 0}, room=8, cost=10_000_000)(
        held, factors, mid, slope, part
    )[0]
    return call(
        outer_kernel,
        [BLOCK, HELD, MID, SLOPE],
        [VMEM] * 8,
        [pltpu.VMEM((3, 2 * INNER, 2 * LANES), jnp.float32), pltpu.SemaphoreType.DMA((3,))],
        aliases={0: 1, 1: 2, 2: 3},
        room=8,
        out_specs=[HBM] + [VMEM] * 3,
    )(held, mid, slope, part, factors, own_row, down_b, down_a)[0]


def solution(mesh):
    return jax.shard_map(
        body,
        mesh=mesh,
        in_specs=(P(None, "gy", "gx"), P("gy", "gx"), P(), P()),
        out_specs=P(None, "gy", "gx"),
        check_vma=False,
    )
```

profile of v0, /device:TPU:249, one launch (start us, length us, event | category | flops | bytes accessed | tf_op | source)
XLA Modules:
  0.0 25.0 jit_solution(14995240811483314410)
XLA Ops:
  0.0 1.4 %shard_map.46 = (f32[16,128]{1,0:T(8,128)S(1)}, f32[16,128]{1,0:T(8,128)S(1)}, f32[16,128]{1,0:T(8,128)S(1)}, f32[12,160,128]{2,1,0:T(8,128)S(1)}) custom-call(f32[3,128,256]{2,1,0:T(8,128)} %water.1, f32[128,256]{1,0:T(8,128)} %bed.1), custom_call_target="tpu_custom_call" | custom-call | tf_op jit(solution)/shard_map/pallas_call | solution.py:412
  1.4 5.2 %collective-permute-start = (f32[16,128]{1,0:T(8,128)S(1)}, f32[16,128]{1,0:T(8,128)S(1)}, u32[]{:S(2)}, u32[]{:S(2)}) collective-permute-start(f32[16,128]{1,0:T(8,128)S(1)} %get-tuple-element.25), channel_id=1, source_target_pairs={{16,32},{32,16},{48,64},{64,48},{80,96},{96,80},{112,128},{128,112... | collective-permute-start | bytes 24584 | tf_op jit(solution)/shard_map/ppermute | solution.py:49
  6.5 1.9 %collective-permute-start.1 = (f32[16,128]{1,0:T(8,128)S(1)}, f32[16,128]{1,0:T(8,128)S(1)}, u32[]{:S(2)}, u32[]{:S(2)}) collective-permute-start(f32[16,128]{1,0:T(8,128)S(1)} %get-tuple-element.26), channel_id=1, source_target_pairs={{0,16},{16,0},{32,48},{48,32},{64,80},{80,64},{96,112},{112,96},{1... | collective-permute-start | bytes 24584 | tf_op jit(solution)/shard_map/ppermute | solution.py:49
  8.5 1.0 %shard_map.47 = (f32[21,8,128]{2,1,0:T(8,128)S(1)}, f32[8,160,128]{2,1,0:T(8,128)S(1)}) custom-call(f32[12,160,128]{2,1,0:T(8,128)S(1)} %get-tuple-element.23.held.held_in, s32[1,16,64]{2,1,0:T(8,128)} %active.1, s32[16,64]{1,0:T(8,128)} %rough.1), custom_call_target="tpu_custom_call" | custom-call | flops 4000000 | bytes 4000000 | tf_op jit(solution)/shard_map/pallas_call | solution.py:420
  9.5 0.0 collective-permute-done.got_b
  9.5 1.5 %collective-permute-done.1.got_a = f32[16,128]{1,0:T(8,128)S(1)} collective-permute-done((f32[16,128]{1,0:T(8,128)S(1)}, f32[16,128]{1,0:T(8,128)S(1)}, u32[]{:S(2)}, u32[]{:S(2)}) %collective-permute-start.1) | collective-permute-done | bytes 8224 | tf_op jit(solution)/shard_map/ppermute | solution.py:49
  10.9 0.2 shard_map.48
  11.2 2.8 %shard_map.49 = (f32[9,160,128]{2,1,0:T(8,128)S(1)}, f32[4,160,128]{2,1,0:T(8,128)S(1)}, f32[3,128,256]{2,1,0:T(8,128)S(1)}, f32[16,384]{1,0:T(8,128)S(1)}) custom-call(f32[12,160,128]{2,1,0:T(8,128)S(1)} %get-tuple-element.28.held.held_in, f32[21,8,128]{2,1,0:T(8,128)S(1)} %get-tuple-element.27.after.factors, ...), custom_call_target="tpu_custom_call", output_to_operand_aliasing={{3}: (3, {})} | custom-call | flops 10000000 | bytes 10000000 | tf_op jit(solution)/shard_map/pallas_call | solution.py:438
  14.0 2.9 %collective-permute-start.3 = (f32[16,384]{1,0:T(8,128)S(1)}, f32[16,384]{1,0:T(8,128)S(1)}, u32[]{:S(2)}, u32[]{:S(2)}) collective-permute-start(f32[16,384]{1,0:T(8,128)S(1)} %get-tuple-element.39), channel_id=1, source_target_pairs={{0,1},{1,0},{2,3},{3,2},{4,5},{5,4},{6,7},{7,6},{8,9},{9,8},{10,11... | collective-permute-start | bytes 73736 | tf_op jit(solution)/shard_map/ppermute | solution.py:49
  16.9 5.1 %collective-permute-start.2 = (f32[16,384]{1,0:T(8,128)S(1)}, f32[16,384]{1,0:T(8,128)S(1)}, u32[]{:S(2)}, u32[]{:S(2)}) collective-permute-start(f32[16,384]{1,0:T(8,128)S(1)} %get-tuple-element.38), channel_id=1, source_target_pairs={{1,2},{2,1},{3,4},{4,3},{5,6},{6,5},{7,8},{8,7},{9,10},{10,9},{11,... | collective-permute-start | bytes 73736 | tf_op jit(solution)/shard_map/ppermute | solution.py:49
  22.0 0.0 collective-permute-done.3.got_a
  22.0 1.5 %collective-permute-done.2.got_b = f32[16,384]{1,0:T(8,128)S(1)} collective-permute-done((f32[16,384]{1,0:T(8,128)S(1)}, f32[16,384]{1,0:T(8,128)S(1)}, u32[]{:S(2)}, u32[]{:S(2)}) %collective-permute-start.2) | collective-permute-done | bytes 24608 | tf_op jit(solution)/shard_map/ppermute | solution.py:49
  23.5 1.5 %shard_map.52 = (f32[3,128,256]{2,1,0:T(8,128)}, f32[12,160,128]{2,1,0:T(8,128)S(1)}, f32[9,160,128]{2,1,0:T(8,128)S(1)}, f32[4,160,128]{2,1,0:T(8,128)S(1)}) custom-call(f32[12,160,128]{2,1,0:T(8,128)S(1)} %get-tuple-element.28.held.held_in, ...), custom_call_target="tpu_custom_call", output_to_operand_aliasing={{1}: (0, {}), {2}: (1, {}), {3}: (2, {})} | custom-call | tf_op jit(solution)/shard_map/pallas_call | solution.py:454
  (2 shorter events, 0.0 us)
Async XLA Ops:
  1.4 8.1 %collective-permute-start = (f32[16,128]{1,0:T(8,128)S(1)}, f32[16,128]{1,0:T(8,128)S(1)}, u32[]{:S(2)}, u32[]{:S(2)}) collective-permute-start(f32[16,128]{1,0:T(8,128)S(1)} %get-tuple-element.25), channel_id=1, source_target_pairs={{16,32},{32,16},{48,64},{64,48},{80,96},{96,80},{112,128},{128,112... | collective-permute-start | bytes 24584 | tf_op jit(solution)/shard_map/ppermute | solution.py:49
  6.5 4.4 %collective-permute-start.1 = (f32[16,128]{1,0:T(8,128)S(1)}, f32[16,128]{1,0:T(8,128)S(1)}, u32[]{:S(2)}, u32[]{:S(2)}) collective-permute-start(f32[16,128]{1,0:T(8,128)S(1)} %get-tuple-element.26), channel_id=1, source_target_pairs={{0,16},{16,0},{32,48},{48,32},{64,80},{80,64},{96,112},{112,96},{1... | collective-permute-start | bytes 24584 | tf_op jit(solution)/shard_map/ppermute | solution.py:49
  14.0 8.0 %collective-permute-start.3 = (f32[16,384]{1,0:T(8,128)S(1)}, f32[16,384]{1,0:T(8,128)S(1)}, u32[]{:S(2)}, u32[]{:S(2)}) collective-permute-start(f32[16,384]{1,0:T(8,128)S(1)} %get-tuple-element.39), channel_id=1, source_target_pairs={{0,1},{1,0},{2,3},{3,2},{4,5},{5,4},{6,7},{7,6},{8,9},{9,8},{10,11... | collective-permute-start | bytes 73736 | tf_op jit(solution)/shard_map/ppermute | solution.py:49
  16.9 6.6 %collective-permute-start.2 = (f32[16,384]{1,0:T(8,128)S(1)}, f32[16,384]{1,0:T(8,128)S(1)}, u32[]{:S(2)}, u32[]{:S(2)}) collective-permute-start(f32[16,384]{1,0:T(8,128)S(1)} %get-tuple-element.38), channel_id=1, source_target_pairs={{1,2},{2,1},{3,4},{4,3},{5,6},{6,5},{7,8},{8,7},{9,10},{10,9},{11,... | collective-permute-start | bytes 73736 | tf_op jit(solution)/shard_map/ppermute | solution.py:49
where the time goes:
time: 25.3 us; the launch traced here: 25 us
  starting transfers between devices  15.1 us (60%)
  Pallas kernels  6.85 us (27%)
  waiting for transfers between devices  2.92 us (12%)
    ppermute x4, starting transfers between devices, swap(): return lax.ppermute(x, axis, pairs)  15.1 us
    ppermute x4, waiting for transfers between devices, swap(): return lax.ppermute(x, axis, pairs)  2.92 us
    pallas_call x1, Pallas kernels, body(): call(odd_kernel, [MID, SLOPE, BLOCK, BAND], [VMEM] * 4, aliases={3: 3}, r...  2.76 us
    pallas_call x1, Pallas kernels, body(): call(outer_kernel, [BLOCK, HELD, MID, SLOPE], [VMEM] * 8, [pltpu.VMEM((3,...  1.46 us
    pallas_call x1, Pallas kernels, body(): call(strips_kernel, [STRIP, STRIP, STRIP, HELD], [HBM] * 2, [pltpu.Semaph...  1.36 us
    pallas_call x1, Pallas kernels, body(): call(ahead_kernel, [FACTORS, KNOWN], [VMEM, HBM, HBM], [pltpu.SMEM((1, 16...  1 us
  transfers between devices with their start and end apart: 4, of which 2 were waited for; matrix products, arithmetic and copies ran while one was open for 0% of the time, Pallas kernels for 4%

commit v1 on v0

--- a/solution.py
+++ b/solution.py
@@ -24,8 +24,8 @@
 DRAG_SCALE = TIME_STEP * GRAVITY
 SMALLEST = 1.1754944e-38
 
-OWN, ABOVE, BELOW = (0, 1, 2), (3, 4, 2), (5, 6, 2)
-REGIONS = 7
+OWN, EDGES = (0, 1, 2), (3, 4, 2)
+REGIONS = 5
 
 VMEM = pl.BlockSpec(memory_space=pltpu.VMEM)
 HBM = pl.BlockSpec(memory_space=pltpu.HBM)
@@ -38,7 +38,8 @@
 STRIP = (16, LANES)
 BAND = (16, 3 * LANES)
 BLOCK = (3, ROWS, 2 * LANES)
-INNER = 16
+EDGE = 8
+HALF = 8
 
 
 def swap(x, axis, odd):
@@ -95,23 +96,18 @@
     for copy in copies:
         copy.start()
 
-    def keep_drag(c):
+    def ahead(c, previous):
+        rows = pl.ds(row_of(c), 8)
         load = loader(held, c)
-        for t in range(2):
-            known[6 + t, pl.ds(row_of(c), 8), :] = drag(*(load(f, t, 0) for f in range(3)))
-
-    def ahead(c, previous):
-        faces = row_faces(loader(held, c), range(2))
+        faces = row_faces(load, range(2))
         over = upper_faces(previous, faces)
         for t in range(2):
             for i in range(3):
-                known[2 * i + t, pl.ds(row_of(c), 8), :] = faces[t][i] - over[t][i]
-        keep_drag(c)
+                known[2 * i + t, rows, :] = faces[t][i] - over[t][i]
+            known[6 + t, rows, :] = drag(*(load(f, t, 0) for f in range(3)))
         return faces
 
-    keep_drag(1)
-    lax.fori_loop(2, 16, ahead, row_faces(loader(held, 1), range(2)), unroll=2)
-    keep_drag(16)
+    lax.fori_loop(1, 17, ahead, no_faces(2), unroll=4)
     for copy in copies:
         copy.wait()
 
@@ -125,16 +121,18 @@
         fine = jnp.where(level == 0, squares[0], squares[1])
         return FLUX_SCALE * on, BED_SCALE * on, jnp.where(level < 2, fine, coarse) * on
 
-    low = lane_ids(8) < 64
-    sites = [(0, 0), (0, 1), None, (-1, 0), (-1, 1), (1, 0), (1, 1)]
-    for region, site in enumerate(sites):
-        if site is None:
-            ahead, behind = tile_of(0, 2), tile_of(0, -1)
-            values = [jnp.where(low, a, b) for a, b in zip(ahead, behind)]
-        else:
-            values = [jnp.full((8, LANES), v, jnp.float32) for v in tile_of(*site)]
+    def keep(region, values):
         for i, v in enumerate(values):
-            factors[3 * region + i] = v
+            factors[3 * region + i] = jnp.broadcast_to(v, (8, LANES))
+
+    rows, low = row_ids(), lane_ids(8) < 64
+    for t in range(2):
+        own, above, below = tile_of(0, t), tile_of(-1, t), tile_of(1, t)
+        keep(OWN[t], own)
+        edges = [jnp.where(rows < 4, b, a) for a, b in zip(above, below)]
+        outside = jnp.logical_and(rows >= 2, rows < 6)
+        keep(EDGES[t], [jnp.where(outside, e, o) for e, o in zip(edges, own)])
+    keep(RIM, [jnp.where(low, a, b) for a, b in zip(tile_of(0, 2), tile_of(0, -1))])
 
 
 def rows_kernel(held_in, own_b, got_b, got_a, after, msg_b, msg_a, keep_b, held, stage):
@@ -232,12 +230,16 @@
         return out
 
 
-def row_faces(load, tiles):
+def row_faces(load, tiles, shift=0):
     out = []
     for t in tiles:
-        sides = [side_states(*(load(f, t, k) for k in (-1, 0, 1, 2))) for f in (0, 2, 1)]
+        sides = [side_states(*(load(f, t, k + shift) for k in (-1, 0, 1, 2))) for f in (0, 2, 1)]
         out.append(rusanov([s[0] for s in sides], [s[1] for s in sides]))
     return out
+
+
+def no_faces(count):
+    return [(jnp.zeros((8, LANES), jnp.float32),) * 3] * count
 
 
 def upper_faces(previous, faces):
@@ -248,9 +250,12 @@
     ]
 
 
+def differences(faces, over):
+    return [[n - o for n, o in zip(*pair)] for pair in zip(faces, over)]
+
+
 def row_of(c):
-    at = 8 * c + TOP - 8
-    return at if isinstance(c, int) else pl.multiple_of(at, 8)
+    return pl.multiple_of(8 * c + TOP - 8, 8)
 
 
 def loader(ref, c):
@@ -258,107 +263,120 @@
     return lambda f, t, k: ref[3 * f + t, pl.ds(base + k, 8), :]
 
 
-def first_stage(ring, held, factors, mid, slope, regions, c, previous, known=None):
-    rows = pl.ds(row_of(c), 8)
-    load = loader(held, c)
-    faces = row_faces(load, range(3) if known is None else [RIM])
-    over = upper_faces(previous, faces)
-    downs = [[n - o for n, o in zip(*pair)] for pair in zip(faces, over)]
-    if known is not None:
-        downs = [[known[2 * i + t, rows, :] for i in range(3)] for t in range(2)] + downs
+def pair_of(ref, e, low, high):
+    first, then = ref[e, low : low + 8, :], ref[e, high - 4 : high + 4, :]
+    return jnp.where(row_ids() < 4, first, then)
+
+
+def section(ring, load, downs, factors, regions, drags):
     h, p, r, b = ([load(f, t, 0) for t in range(3)] for f in range(4))
     along = ring.rates(h, p, r, 3)
     to_left, to_right = ring.right(b), ring.left(b)
+    states, slopes = [], []
     for t in range(3):
         flux, bed, rub = (factors[3 * regions[t] + i] for i in range(3))
         bed_x = bed * (to_right[t] - to_left[t])
         bed_y = bed * (load(3, t, 1) - load(3, t, -1))
-        if t != RIM:
-            slope[t, rows, :] = bed_x
-            slope[2 + t, rows, :] = bed_y
-        if known is None or t == RIM:
-            res = rub * drag(h[t], p[t], r[t])
-        else:
-            res = rub * known[6 + t, rows, :]
+        res = rub * (drag(h[t], p[t], r[t]) if drags[t] is None else drags[t])
         down = downs[t]
-        mid[t, rows, :] = h[t] - flux * (along[0][t] + down[0])
-        mid[3 + t, rows, :] = p[t] - (
-            flux * (along[1][t] + down[2]) + (h[t] * bed_x + res * p[t])
+        states.append(
+            (
+                h[t] - flux * (along[0][t] + down[0]),
+                p[t] - (flux * (along[1][t] + down[2]) + (h[t] * bed_x + res * p[t])),
+                r[t] - (flux * (along[2][t] + down[1]) + (h[t] * bed_y + res * r[t])),
+            )
         )
-        mid[6 + t, rows, :] = r[t] - (
-            flux * (along[2][t] + down[1]) + (h[t] * bed_y + res * r[t])
-        )
-    return faces
-
-
-def second_stage(ring, held, factors, mid, slope, out, place, c, previous):
-    rows = pl.ds(row_of(c), 8)
-    load = loader(mid, c)
-    faces = row_faces(load, range(2))
-    over = upper_faces(previous, faces)
+        slopes.append((bed_x, bed_y))
+    return states, slopes
+
+
+def result(ring, load, downs, factors, slope_at, start_at):
     h, p, r = ([load(f, t, 0) for t in range(3)] for f in range(3))
     along = ring.rates(h, p, r, 2)
+    out = []
     for t in range(2):
-        flux, _, rub = (factors[3 * OWN[t] + i] for i in range(3))
+        flux, rub = factors[3 * OWN[t]], factors[3 * OWN[t] + 2]
         res = rub * drag(h[t], p[t], r[t])
-        down = [n - o for n, o in zip(faces[t], over[t])]
+        down = downs[t]
         change = (
             flux * (along[0][t] + down[0]),
-            flux * (along[1][t] + down[2]) + (h[t] * slope[t, rows, :] + res * p[t]),
-            flux * (along[2][t] + down[1]) + (h[t] * slope[2 + t, rows, :] + res * r[t]),
+            flux * (along[1][t] + down[2]) + (h[t] * slope_at(t) + res * p[t]),
+            flux * (along[2][t] + down[1]) + (h[t] * slope_at(2 + t) + res * r[t]),
         )
-        for f, v in enumerate((h, p, r)):
-            start = held[3 * f + t, rows, :]
-            out[f, pl.ds(place, 8), pl.ds(t * LANES, LANES)] = 0.5 * ((start + v[t]) - change[f])
-    return faces
+        out.append(
+            [0.5 * ((start_at(3 * f + t) + v[t]) - change[f]) for f, v in enumerate((h, p, r))]
+        )
+    return out
 
 
 def inner_section(held, factors, known, mid, slope):
     ring = Ring()
 
-    def first(c, previous):
-        return first_stage(ring, held, factors, mid, slope, OWN, c, previous, known)
-
-    lax.fori_loop(2, 16, first, row_faces(loader(held, 1), [RIM]), unroll=2)
-
-
-def inner_result(held, factors, mid, slope, part):
+    def step(c, previous):
+        rows = pl.ds(row_of(c), 8)
+        load = loader(held, c)
+        faces = row_faces(load, [RIM])
+        downs = [[known[2 * i + t, rows, :] for i in range(3)] for t in range(2)]
+        downs += differences(faces, upper_faces(previous, faces))
+        drags = [known[6, rows, :], known[7, rows, :], None]
+        states, slopes = section(ring, load, downs, factors, OWN, drags)
+        for t in range(3):
+            for f in range(3):
+                mid[3 * f + t, rows, :] = states[t][f]
+            if t != RIM:
+                slope[t, rows, :], slope[2 + t, rows, :] = slopes[t]
+        return faces
+
+    lax.fori_loop(1, 17, step, no_faces(1), unroll=4)
+
+
+def inner_result(held, factors, mid, slope, part, first, last):
     ring = Ring()
 
-    def second(c, previous):
-        place = pl.multiple_of(8 * c - 8, 8)
-        return second_stage(ring, held, factors, mid, slope, part, place, c, previous)
-
-    lax.fori_loop(3, 15, second, row_faces(loader(mid, 2), range(2)), unroll=4)
+    def step(c, previous):
+        rows = pl.ds(row_of(c), 8)
+        load = loader(mid, c)
+        faces = row_faces(load, range(2))
+        downs = differences(faces, upper_faces(previous, faces))
+        values = result(
+            ring, load, downs, factors, lambda i: slope[i, rows, :], lambda e: held[e, rows, :]
+        )
+        place = pl.ds(pl.multiple_of(8 * c - 8, 8), 8)
+        for t in range(2):
+            for f in range(3):
+                part[f, place, pl.ds(t * LANES, LANES)] = values[t][f]
+        return faces
+
+    before = no_faces(2) if first == 1 else row_faces(loader(mid, first - 1), range(2))
+    lax.fori_loop(first, last + 1, step, before, unroll=4)
 
 
 def odd_kernel(held, factors, known, msg_in, mid, slope, part, msg):
     @pl.when(lax.rem(lax.axis_index("gy"), 2) == 1)
     def _():
         inner_section(held, factors, known, mid, slope)
-        inner_result(held, factors, mid, slope, part)
-
-
-def even_kernel(held, factors, known, msg_in, mid_in, slope_in, mid, slope, msg):
+        inner_result(held, factors, mid, slope, part, 1, HALF)
+
+
+def even_kernel(held, factors, known, msg_in, mid_in, slope_in, part_in, mid, slope, part, msg):
     @pl.when(lax.rem(lax.axis_index("gy"), 2) == 0)
     def _():
         inner_section(held, factors, known, mid, slope)
+        inner_result(held, factors, mid, slope, part, 1, HALF)
 
 
 def rest_kernel(held, factors, mid, slope, part_in, part):
-    @pl.when(lax.rem(lax.axis_index("gy"), 2) == 0)
-    def _():
-        inner_result(held, factors, mid, slope, part)
+    inner_result(held, factors, mid, slope, part, HALF + 1, 16)
 
 
 def outer_kernel(
     held_in, mid_in, slope_in, part, factors, own_b, got_b, got_a, out, held, mid, slope, edge, sems
 ):
-    inner = pl.ds(INNER, ROWS - 2 * INNER)
+    inner = pl.ds(EDGE, ROWS - 2 * EDGE)
     copies = [pltpu.make_async_copy(part.at[:, inner, :], out.at[:, inner, :], sems.at[0])]
     for i in range(2):
-        src, dst = pl.ds(i * INNER, INNER), pl.ds(i * (ROWS - INNER), INNER)
-        copies.append(pltpu.make_async_copy(edge.at[:, src, :], out.at[:, dst, :], sems.at[1 + i]))
+        rows = pl.ds(i * (ROWS - EDGE), EDGE)
+        copies.append(pltpu.make_async_copy(edge.at[i], out.at[:, rows, :], sems.at[1 + i]))
     copies[0].start()
     gy, ny = lax.axis_index("gy"), lax.axis_size("gy")
     even_y = lax.rem(gy, 2) == 0
@@ -376,20 +394,46 @@
             held[3 * f + t, TOP + ROWS : TOP + ROWS + 4, :] = jnp.where(even_y, a, b)
 
     ring = Ring()
-    zero = jnp.zeros((8, LANES), jnp.float32)
-
-    def first(c, regions, previous):
-        return first_stage(ring, held, factors, mid, slope, regions, c, previous)
-
-    def second(c, place, previous):
-        return second_stage(ring, held, factors, mid, slope, edge, place, c, previous)
-
-    first(1, OWN, first(0, ABOVE, [(zero, zero, zero)] * 3))
-    first(17, BELOW, first(16, OWN, row_faces(loader(held, 15), range(3))))
-    second(2, 8, second(1, 0, row_faces(loader(mid, 0), range(2))))
-    copies[1].start()
-    second(16, 24, second(15, 16, row_faces(loader(mid, 14), range(2))))
-    copies[2].start()
+    end = TOP + ROWS
+
+    def load(f, t, k):
+        return pair_of(held, 3 * f + t, end - 2 + k, TOP - 2 + k)
+
+    downs = differences(row_faces(load, range(3)), row_faces(load, range(3), -1))
+    states, slopes = section(ring, load, downs, factors, EDGES, [None] * 3)
+
+    def put(ref, e, v):
+        ref[e, end - 2 : end + 2, :] = v[0:4, :]
+        ref[e, TOP - 2 : TOP + 2, :] = v[4:8, :]
+
+    for t in range(3):
+        for f in range(3):
+            put(mid, 3 * f + t, states[t][f])
+        if t != RIM:
+            put(slope, t, slopes[t][0])
+            put(slope, 2 + t, slopes[t][1])
+
+    def load_mid(f, t, k):
+        return pair_of(mid, 3 * f + t, end - 4 + k, TOP + k)
+
+    downs = differences(row_faces(load_mid, range(2)), row_faces(load_mid, range(2), -1))
+    values = result(
+        ring,
+        load_mid,
+        downs,
+        factors,
+        lambda i: pair_of(slope, i, end - 4, TOP),
+        lambda e: pair_of(held, e, end - 4, TOP),
+    )
+    upper = row_ids() < 4
+    for t in range(2):
+        cols = pl.ds(t * LANES, LANES)
+        for f in range(3):
+            v = pltpu.roll(values[t][f], 4, 0)
+            edge[0, f, :, cols] = jnp.where(upper, v, part[f, 0:EDGE, cols])
+            edge[1, f, :, cols] = jnp.where(upper, part[f, ROWS - EDGE : ROWS, cols], v)
+    for copy in copies[1:]:
+        copy.start()
     for copy in copies:
         copy.wait()
 
@@ -439,14 +483,14 @@
         odd_kernel, [MID, SLOPE, BLOCK, BAND], [VMEM] * 4, aliases={3: 3}, room=8, cost=10_000_000
     )(held, factors, known, row_b)
     down_b = swap(row_b, "gy", 1)
-    mid, slope, row_a = call(
+    mid, slope, part, row_a = call(
         even_kernel,
-        [MID, SLOPE, BAND],
-        [VMEM] * 6,
-        aliases={4: 0, 5: 1, 3: 2},
+        [MID, SLOPE, BLOCK, BAND],
+        [VMEM] * 7,
+        aliases={4: 0, 5: 1, 6: 2, 3: 3},
         room=8,
         cost=10_000_000,
-    )(held, factors, known, row_a, mid, slope)
+    )(held, factors, known, row_a, mid, slope, part)
     down_a = swap(row_a, "gy", 0)
     part = call(rest_kernel, [BLOCK], [VMEM] * 5, aliases={4: 0}, room=8, cost=10_000_000)(
         held, factors, mid, slope, part
@@ -455,7 +499,7 @@
         outer_kernel,
         [BLOCK, HELD, MID, SLOPE],
         [VMEM] * 8,
-        [pltpu.VMEM((3, 2 * INNER, 2 * LANES), jnp.float32), pltpu.SemaphoreType.DMA((3,))],
+        [pltpu.VMEM((2, 3, EDGE, 2 * LANES), jnp.float32), pltpu.SemaphoreType.DMA((3,))],
         aliases={0: 1, 1: 2, 2: 3},
         room=8,
         out_specs=[HBM] + [VMEM] * 3,

time: 25.3 us -> 25.5 us (level)
  starting transfers between devices: 15.1 us -> 16.2 us
  waiting for transfers between devices: 2.92 us -> 2.18 us
    ppermute x4, starting transfers between devices: 15.1 us -> 16.2 us  [swap(): return lax.ppermute(x, axis, pairs)]
    ppermute x4, waiting for transfers between devices: 2.92 us -> 2.18 us  [swap(): return lax.ppermute(x, axis, pairs)]
    pallas_call x1, Pallas kernels: 0.02 us -> 0.75 us  [body(): call(rest_kernel, [BLOCK], [VMEM] * 5, aliases={4: 0}, room=8, cost=10000...]
    pallas_call x1, Pallas kernels: 2.76 us -> 2.25 us  [body(): call(odd_kernel, [MID, SLOPE, BLOCK, BAND], [VMEM] * 4, aliases={3: 3}, r...]
    pallas_call x2, Pallas kernels: 1.48 us -> 1.06 us  [the longest x1 1.04 us: body(): call(outer_kernel, [BLOCK, HELD, MID, SLOPE], [VMEM] * 8, [pltpu.VMEM((2,...]
  transfers between devices with their start and end apart: 4 -> 4, of which waited for: 2 -> 2; matrix products, arithmetic and copies ran while one was open for 0% -> 0% of each run, Pallas kernels for 4% -> 7%
where the time goes in v1:
time: 25.5 us; the launch traced here: 25.1 us
  starting transfers between devices  16.2 us (64%)
  Pallas kernels  6.66 us (26%)
  waiting for transfers between devices  2.18 us (9%)
    ppermute x4, starting transfers between devices, swap(): return lax.ppermute(x, axis, pairs)  16.2 us
    pallas_call x1, Pallas kernels, body(): call(odd_kernel, [MID, SLOPE, BLOCK, BAND], [VMEM] * 4, aliases={3: 3}, r...  2.25 us
    ppermute x4, waiting for transfers between devices, swap(): return lax.ppermute(x, axis, pairs)  2.18 us
    pallas_call x1, Pallas kernels, body(): call(strips_kernel, [STRIP, STRIP, STRIP, HELD], [HBM] * 2, [pltpu.Semaph...  1.36 us
    pallas_call x1, Pallas kernels, body(): call(outer_kernel, [BLOCK, HELD, MID, SLOPE], [VMEM] * 8, [pltpu.VMEM((2,...  1.04 us
    pallas_call x1, Pallas kernels, body(): call(ahead_kernel, [FACTORS, KNOWN], [VMEM, HBM, HBM], [pltpu.SMEM((1, 16...  1 us
    pallas_call x1, Pallas kernels, body(): call(rest_kernel, [BLOCK], [VMEM] * 5, aliases={4: 0}, room=8, cost=10000...  0.75 us
  transfers between devices with their start and end apart: 4, of which 2 were waited for; matrix products, arithmetic and copies ran while one was open for 0% of the time, Pallas kernels for 7%

profile of v1, /device:TPU:249, one launch (start us, length us, event | category | flops | bytes accessed | tf_op | source)
XLA Modules:
  0.0 25.1 jit_solution(2691400278520253705)
XLA Ops:
  0.0 1.4 %shard_map.46 = (f32[16,128]{1,0:T(8,128)S(1)}, f32[16,128]{1,0:T(8,128)S(1)}, f32[16,128]{1,0:T(8,128)S(1)}, f32[12,160,128]{2,1,0:T(8,128)S(1)}) custom-call(f32[3,128,256]{2,1,0:T(8,128)} %water.1, f32[128,256]{1,0:T(8,128)} %bed.1), custom_call_target="tpu_custom_call" | custom-call | tf_op jit(solution)/shard_map/pallas_call | solution.py:456
  1.4 5.2 %collective-permute-start = (f32[16,128]{1,0:T(8,128)S(1)}, f32[16,128]{1,0:T(8,128)S(1)}, u32[]{:S(2)}, u32[]{:S(2)}) collective-permute-start(f32[16,128]{1,0:T(8,128)S(1)} %get-tuple-element.26), channel_id=1, source_target_pairs={{16,32},{32,16},{48,64},{64,48},{80,96},{96,80},{112,128},{128,112... | collective-permute-start | bytes 24584 | tf_op jit(solution)/shard_map/ppermute | solution.py:50
  6.5 1.9 %collective-permute-start.1 = (f32[16,128]{1,0:T(8,128)S(1)}, f32[16,128]{1,0:T(8,128)S(1)}, u32[]{:S(2)}, u32[]{:S(2)}) collective-permute-start(f32[16,128]{1,0:T(8,128)S(1)} %get-tuple-element.27), channel_id=1, source_target_pairs={{0,16},{16,0},{32,48},{48,32},{64,80},{80,64},{96,112},{112,96},{1... | collective-permute-start | bytes 24584 | tf_op jit(solution)/shard_map/ppermute | solution.py:50
  8.5 1.0 %shard_map.47 = (f32[15,8,128]{2,1,0:T(8,128)S(1)}, f32[8,160,128]{2,1,0:T(8,128)S(1)}) custom-call(f32[12,160,128]{2,1,0:T(8,128)S(1)} %get-tuple-element.24.held.held_in, s32[1,16,64]{2,1,0:T(8,128)} %active.1, s32[16,64]{1,0:T(8,128)} %rough.1), custom_call_target="tpu_custom_call" | custom-call | flops 4000000 | bytes 4000000 | tf_op jit(solution)/shard_map/pallas_call | solution.py:464
  9.5 0.0 collective-permute-done.got_b
  9.5 1.5 %collective-permute-done.1.got_a = f32[16,128]{1,0:T(8,128)S(1)} collective-permute-done((f32[16,128]{1,0:T(8,128)S(1)}, f32[16,128]{1,0:T(8,128)S(1)}, u32[]{:S(2)}, u32[]{:S(2)}) %collective-permute-start.1) | collective-permute-done | bytes 8224 | tf_op jit(solution)/shard_map/ppermute | solution.py:50
  10.9 0.2 shard_map.48
  11.2 2.2 %shard_map.49 = (f32[9,160,128]{2,1,0:T(8,128)S(1)}, f32[4,160,128]{2,1,0:T(8,128)S(1)}, f32[3,128,256]{2,1,0:T(8,128)S(1)}, f32[16,384]{1,0:T(8,128)S(1)}) custom-call(f32[12,160,128]{2,1,0:T(8,128)S(1)} %get-tuple-element.29.held.held_in, f32[15,8,128]{2,1,0:T(8,128)S(1)} %get-tuple-element.28.after.factors, ...), custom_call_target="tpu_custom_call", output_to_operand_aliasing={{3}: (3, {})} | custom-call | flops 10000000 | bytes 10000000 | tf_op jit(solution)/shard_map/pallas_call | solution.py:482
  13.5 4.0 %collective-permute-start.3 = (f32[16,384]{1,0:T(8,128)S(1)}, f32[16,384]{1,0:T(8,128)S(1)}, u32[]{:S(2)}, u32[]{:S(2)}) collective-permute-start(f32[16,384]{1,0:T(8,128)S(1)} %get-tuple-element.41), channel_id=1, source_target_pairs={{0,1},{1,0},{2,3},{3,2},{4,5},{5,4},{6,7},{7,6},{8,9},{9,8},{10,11... | collective-permute-start | bytes 73736 | tf_op jit(solution)/shard_map/ppermute | solution.py:50
  17.5 5.1 %collective-permute-start.2 = (f32[16,384]{1,0:T(8,128)S(1)}, f32[16,384]{1,0:T(8,128)S(1)}, u32[]{:S(2)}, u32[]{:S(2)}) collective-permute-start(f32[16,384]{1,0:T(8,128)S(1)} %get-tuple-element.40), channel_id=1, source_target_pairs={{1,2},{2,1},{3,4},{4,3},{5,6},{6,5},{7,8},{8,7},{9,10},{10,9},{11,... | collective-permute-start | bytes 73736 | tf_op jit(solution)/shard_map/ppermute | solution.py:50
  22.6 0.8 %shard_map.51.part = f32[3,128,256]{2,1,0:T(8,128)S(1)} custom-call(f32[12,160,128]{2,1,0:T(8,128)S(1)} %get-tuple-element.29.held.held_in, f32[15,8,128]{2,1,0:T(8,128)S(1)} %get-tuple-element.28.after.factors, f32[9,160,128]{2,1,0:T(8,128)S(1)} %get-tuple-element.36.mid.mid_in, ...), custom_call_target="tpu_custom_call", output_to_operand_aliasing={{}: (4, {})} | custom-call | flops 10000000 | bytes 10000000 | tf_op jit(solution)/shard_map/pallas_call | solution.py:495
  23.4 0.0 collective-permute-done.3.got_a
  23.4 0.7 %collective-permute-done.2.got_b = f32[16,384]{1,0:T(8,128)S(1)} collective-permute-done((f32[16,384]{1,0:T(8,128)S(1)}, f32[16,384]{1,0:T(8,128)S(1)}, u32[]{:S(2)}, u32[]{:S(2)}) %collective-permute-start.2) | collective-permute-done | bytes 24608 | tf_op jit(solution)/shard_map/ppermute | solution.py:50
  24.1 1.0 %shard_map.52 = (f32[3,128,256]{2,1,0:T(8,128)}, f32[12,160,128]{2,1,0:T(8,128)S(1)}, f32[9,160,128]{2,1,0:T(8,128)S(1)}, f32[4,160,128]{2,1,0:T(8,128)S(1)}) custom-call(f32[12,160,128]{2,1,0:T(8,128)S(1)} %get-tuple-element.29.held.held_in, ...), custom_call_target="tpu_custom_call", output_to_operand_aliasing={{1}: (0, {}), {2}: (1, {}), {3}: (2, {})} | custom-call | tf_op jit(solution)/shard_map/pallas_call | solution.py:498
  (1 shorter events, 0.0 us)
Async XLA Ops:
  1.4 8.1 %collective-permute-start = (f32[16,128]{1,0:T(8,128)S(1)}, f32[16,128]{1,0:T(8,128)S(1)}, u32[]{:S(2)}, u32[]{:S(2)}) collective-permute-start(f32[16,128]{1,0:T(8,128)S(1)} %get-tuple-element.26), channel_id=1, source_target_pairs={{16,32},{32,16},{48,64},{64,48},{80,96},{96,80},{112,128},{128,112... | collective-permute-start | bytes 24584 | tf_op jit(solution)/shard_map/ppermute | solution.py:50
  6.5 4.4 %collective-permute-start.1 = (f32[16,128]{1,0:T(8,128)S(1)}, f32[16,128]{1,0:T(8,128)S(1)}, u32[]{:S(2)}, u32[]{:S(2)}) collective-permute-start(f32[16,128]{1,0:T(8,128)S(1)} %get-tuple-element.27), channel_id=1, source_target_pairs={{0,16},{16,0},{32,48},{48,32},{64,80},{80,64},{96,112},{112,96},{1... | collective-permute-start | bytes 24584 | tf_op jit(solution)/shard_map/ppermute | solution.py:50
  13.5 9.9 %collective-permute-start.3 = (f32[16,384]{1,0:T(8,128)S(1)}, f32[16,384]{1,0:T(8,128)S(1)}, u32[]{:S(2)}, u32[]{:S(2)}) collective-permute-start(f32[16,384]{1,0:T(8,128)S(1)} %get-tuple-element.41), channel_id=1, source_target_pairs={{0,1},{1,0},{2,3},{3,2},{4,5},{5,4},{6,7},{7,6},{8,9},{9,8},{10,11... | collective-permute-start | bytes 73736 | tf_op jit(solution)/shard_map/ppermute | solution.py:50
  17.5 6.6 %collective-permute-start.2 = (f32[16,384]{1,0:T(8,128)S(1)}, f32[16,384]{1,0:T(8,128)S(1)}, u32[]{:S(2)}, u32[]{:S(2)}) collective-permute-start(f32[16,384]{1,0:T(8,128)S(1)} %get-tuple-element.40), channel_id=1, source_target_pairs={{1,2},{2,1},{3,4},{4,3},{5,6},{6,5},{7,8},{8,7},{9,10},{10,9},{11,... | collective-permute-start | bytes 73736 | tf_op jit(solution)/shard_map/ppermute | solution.py:50
